TPU v7x, 512 devices: a whole 4x4x16 slice. The times are simulated.
512 devices in a mesh: ka: 64 (over z_lo, x, core), mu: 8 (over y, z_hi).
Axes of the slice: x: 4, y: 4, z: 16 (z_hi: 2, z_lo: 8; z = z_hi * 8 + z_lo), core: 2. Of those that a mesh axis runs over, the one named last changes fastest.
Arguments:
- vectors: float32 [3, 64, 4096], P(None, 'ka', 'mu'), may hold values from -6 to 6
- phi_val: bfloat16 [64, 64, 2048], P('ka', None, 'mu'), may hold values from -6 to 6
- phi_con: bfloat16 [64, 64, 2048], P('ka', None, 'mu'), may hold values from -6 to 6
- screened: bfloat16 [4, 2048, 2048], P(None, 'mu'), may hold values from -4.5776367e-05 to 4.5776367e-05
- partner: int32 [64, 4], P('ka'), may hold values from 0 to 63, as said below
Outputs:
- result: float32 [3, 64, 4096], P(None, 'ka', 'mu')
Inputs may be any that keep to these rules, and one draw needn't show every extreme that they name: With s = (1, -1, 2, -2) for offsets 0 to 3, partner[k, o] = (k - s[o]) modulo 64; each ka index j holds exactly one k-point, k-point j.
All inputs are finite; a program needn't handle non-finite values.
Results may differ from a plain program's by a relative error of at most 0.0058.
Values may be sent and summed in bfloat16 or wider, within the bound.
A program may use at most 64 MiB of HBM per device.

v0:
```python
import jax
import jax.numpy as jnp
from jax import lax
from jax.sharding import PartitionSpec as P

cycle_steps = (1, -1, 2, -2)


def joined_along(pieces, dim):
    pieces = jnp.moveaxis(pieces, 0, dim)
    shape = pieces.shape
    return pieces.reshape(*shape[:dim], shape[dim] * shape[dim + 1], *shape[dim + 2 :])


def sent_to_all(value, axis):
    copies = jnp.broadcast_to(value, (lax.axis_size(axis), *value.shape))
    return lax.all_to_all(copies, axis, split_axis=0, concat_axis=0, tiled=True)


def collect(value, axis, dim):
    return joined_along(sent_to_all(value, axis), dim)


def passed_along(value, axis, steps):
    count = lax.axis_size(axis)
    pairs = [(source, (source + steps) % count) for source in range(count)]
    return lax.ppermute(value, axis, pairs)


def in_blocks(value, dim, length):
    before, after = (value.shape[:dim], value.shape[dim + 1 :])
    return jnp.moveaxis(value.reshape(*before, length, -1, *after), dim, 0)


def sum_at_owner(value, axis, dim):
    pieces = in_blocks(value, dim, lax.axis_size(axis))
    arrived = lax.all_to_all(pieces, axis, split_axis=0, concat_axis=0, tiled=True)
    return arrived.sum(axis=0)


def local(vectors, phi_val, phi_con, screened, partner):
    local_points = phi_val.shape[0]
    vec_count = vectors.shape[0]
    valence = phi_val.shape[1]
    conduction = phi_con.shape[1]
    vec_coded = vectors.astype(jnp.bfloat16)
    con_home, vec_home = (collect(phi_con, "mu", 2), collect(vec_coded, "mu", 2))
    running_sum = jnp.zeros((vec_count, local_points, valence, conduction), jnp.float32)
    for offset, cycle_step in enumerate(cycle_steps):
        val_far, con_far, vec_far = passed_along((phi_val, con_home, vec_home), "ka", cycle_step)
        slot_index = partner[:, offset] % local_points
        val_sel = jnp.take(val_far, slot_index, axis=0)
        con_sel = jnp.take(con_far, slot_index, axis=0)
        vec_sel = jnp.take(vec_far, slot_index, axis=1).reshape(
            vec_count, local_points, valence, conduction
        )
        kernel = screened[offset]

        def per_vector(vec_single):
            blended = jnp.einsum(
                "kvc,kcn->kvn", vec_single, con_sel, preferred_element_type=jnp.float32
            ).astype(jnp.bfloat16)
            paired = jnp.einsum(
                "kvm,kvn->kmn", val_sel, blended, preferred_element_type=jnp.float32
            )
            weighted = (kernel.astype(jnp.float32)[None] * paired).astype(jnp.bfloat16)
            folded = jnp.einsum(
                "kmn,kcn->kmc", weighted, con_home, preferred_element_type=jnp.float32
            ).astype(jnp.bfloat16)
            return jnp.einsum("kvm,kmc->kvc", phi_val, folded, preferred_element_type=jnp.float32)

        running_sum = running_sum + lax.map(per_vector, vec_sel)
    pair_terms = running_sum.reshape(vec_count, local_points, valence * conduction)
    return sum_at_owner(pair_terms, "mu", 2)


def solution(mesh):
    placed = (
        P(None, "ka", "mu"),
        P("ka", None, "mu"),
        P("ka", None, "mu"),
        P(None, "mu", None),
        P("ka", None),
    )
    return jax.shard_map(
        local, mesh=mesh, in_specs=placed, out_specs=P(None, "ka", "mu"), check_vma=False
    )
```

profile of v0, /device:TPU:8, one launch (start us, length us, event | category | flops | bytes accessed | tf_op | source)
XLA Modules:
  0.0 179.4 jit_solution(17374418134634061375)
XLA Ops:
  0.7 31.5 %all_to_all.15 = bf16[8,3,1,512]{3,1,2,0:T(4,128)(2,1)S(1)} all-to-all(bf16[8,3,1,512]{3,1,2,0:T(4,128)(2,1)S(1)} %broadcast_in_dim.68), channel_id=1, replica_groups=mesh['ka'=64,'mu'=8] {'mu'}, dimensions={0} | all-to-all | bytes 49152 | tf_op jit(solution)/shard_map/all_to_all | solution.py:17
  33.7 4.8 %all-to-all-start.1 = ((bf16[8,1,64,256]{3,2,1,0:T(8,128)(2,1)}), bf16[8,1,64,256]{3,2,1,0:T(8,128)(2,1)S(1)}, u32[]{:S(2)}, u32[]{:S(2)}) async-start(bf16[8,1,64,256]{3,2,1,0:T(8,128)(2,1)} %broadcast_in_dim.69), calls=%async_computation.1 | async-start | bytes 524288 | tf_op jit(solution)/shard_map/all_to_all | solution.py:17
  38.4 7.8 %collective-permute-start.9 = (bf16[3,1,4096]{2,0,1:T(4,128)(2,1)S(1)}, bf16[3,1,4096]{2,0,1:T(4,128)(2,1)S(1)}, u32[]{:S(2)}, u32[]{:S(2)}) collective-permute-start(bf16[3,1,4096]{2,0,1:T(4,128)(2,1)S(1)} %bitcast.242), channel_id=1, source_target_pairs={{0,496},{8,504},{16,0},{24,8},{32,16},{40,24},{48,32},{56,40},{64,... | collective-permute-start | bytes 73736 | tf_op jit(solution)/shard_map/ppermute | solution.py:27
  46.3 2.7 %collective-permute-start.11 = (bf16[1,64,256]{2,1,0:T(8,128)(2,1)}, bf16[1,64,256]{2,1,0:T(8,128)(2,1)}, u32[]{:S(2)}, u32[]{:S(2)}) collective-permute-start(bf16[1,64,256]{2,1,0:T(8,128)(2,1)} %param.14), channel_id=1, source_target_pairs={{0,496},{8,504},{16,0},{24,8},{32,16},{40,24},{48,32},{56,40},{64,... | collective-permute-start | bytes 98312 | tf_op jit(solution)/shard_map/ppermute | solution.py:27
  49.0 3.1 %collective-permute-start.6 = (bf16[3,1,4096]{2,0,1:T(4,128)(2,1)S(1)}, bf16[3,1,4096]{2,0,1:T(4,128)(2,1)S(1)}, u32[]{:S(2)}, u32[]{:S(2)}) collective-permute-start(bf16[3,1,4096]{2,0,1:T(4,128)(2,1)S(1)} %bitcast.243), channel_id=1, source_target_pairs={{0,16},{8,24},{16,32},{24,40},{32,48},{40,56},{48,64},{56,72},{64,... | collective-permute-start | bytes 73736 | tf_op jit(solution)/shard_map/ppermute | solution.py:27
  54.1 12.4 %collective-permute-start.3 = (bf16[3,1,4096]{2,0,1:T(4,128)(2,1)S(1)}, bf16[3,1,4096]{2,0,1:T(4,128)(2,1)}, u32[]{:S(2)}, u32[]{:S(2)}) collective-permute-start(bf16[3,1,4096]{2,0,1:T(4,128)(2,1)S(1)} %bitcast.245), channel_id=1, source_target_pairs={{0,504},{8,0},{16,8},{24,16},{32,24},{40,32},{48,40},{56,48},{64,5... | collective-permute-start | bytes 73736 | tf_op jit(solution)/shard_map/ppermute | solution.py:27
  67.2 2.7 %collective-permute-start.10 = (bf16[1,64,2048]{2,1,0:T(8,128)(2,1)}, bf16[1,64,2048]{2,1,0:T(8,128)(2,1)S(1)}, u32[]{:S(2)}, u32[]{:S(2)}) collective-permute-start(bf16[1,64,2048]{2,1,0:T(8,128)(2,1)} %bitcast.48), channel_id=1, source_target_pairs={{0,496},{8,504},{16,0},{24,8},{32,16},{40,24},{48,32},{56,40},{64,... | collective-permute-start | bytes 786440 | tf_op jit(solution)/shard_map/ppermute | solution.py:27
  69.9 3.6 %fusion.52 = (bf16[1,256,2048]{2,1,0:T(8,128)(2,1)S(1)}, bf16[1,256,2048]{2,1,0:T(8,128)(2,1)S(1)}, bf16[1,256,2048]{2,1,0:T(8,128)(2,1)S(1)}, bf16[1,256,2048]{2,1,0:T(8,128)(2,1)}) fusion(bf16[4,256,2048]{2,1,0:T(8,128)(2,1)} %param.16), kind=kLoop, calls=%fused_computation.62 | loop fusion | bytes 8388608 | tf_op jit(solution)/shard_map/slice | solution.py:57
  73.5 2.3 %copy.30 = bf16[1,256,2048]{1,2,0:T(8,128)(2,1)} copy(bf16[1,256,2048]{2,1,0:T(8,128)(2,1)} %get-tuple-element.244) | data formatting | bytes 2097152
  78.3 3.1 %collective-permute-start.8 = (bf16[1,64,256]{2,1,0:T(8,128)(2,1)}, bf16[1,64,256]{2,1,0:T(8,128)(2,1)S(1)}, u32[]{:S(2)}, u32[]{:S(2)}) collective-permute-start(bf16[1,64,256]{2,1,0:T(8,128)(2,1)} %param.14), channel_id=1, source_target_pairs={{0,16},{8,24},{16,32},{24,40},{32,48},{40,56},{48,64},{56,72},{64,... | collective-permute-start | bytes 98312 | tf_op jit(solution)/shard_map/ppermute | solution.py:27
  81.5 1.9 %collective-permute-start.2 = (bf16[1,64,256]{2,1,0:T(8,128)(2,1)}, bf16[1,64,256]{2,1,0:T(8,128)(2,1)}, u32[]{:S(2)}, u32[]{:S(2)}) collective-permute-start(bf16[1,64,256]{2,1,0:T(8,128)(2,1)} %param.14), channel_id=1, source_target_pairs={{0,8},{8,16},{16,24},{24,32},{32,40},{40,48},{48,56},{56,64},{64,7... | collective-permute-start | bytes 98312 | tf_op jit(solution)/shard_map/ppermute | solution.py:27
  84.3 12.4 %collective-permute-start.5 = (bf16[1,64,256]{2,1,0:T(8,128)(2,1)}, bf16[1,64,256]{2,1,0:T(8,128)(2,1)S(1)}, u32[]{:S(2)}, u32[]{:S(2)}) collective-permute-start(bf16[1,64,256]{2,1,0:T(8,128)(2,1)} %param.14), channel_id=1, source_target_pairs={{0,504},{8,0},{16,8},{24,16},{32,24},{40,32},{48,40},{56,48},{64,5... | collective-permute-start | bytes 98312 | tf_op jit(solution)/shard_map/ppermute | solution.py:27
  101.4 9.7 %while.43 = (s32[]{:T(128)}, f32[3,1,64,64]{2,3,1,0:T(8,128)S(1)}, bf16[256,2048]{0,1:T(8,128)(2,1)}, bf16[3,1,64,64]{3,2,1,0:T(8,128)(2,1)S(1)}, bf16[1,64,2048...) while((s32[]{:T(128)}, f32[3,1,64,64]{2,3,1,0:T(8,128)S(1)}, ...), condition=%wide.region_7.8_spmd, body=%wide.region_6.7_spmd.sunk | while | flops 154812416 | bytes 2277485 | solution.py:72
  101.7 2.1 %fusion.131 = bf16[256,64]{0,1:T(8,128)(2,1)S(1)} fusion(bf16[64,2048]{1,0:T(8,128)(2,1)S(1)} %convolution_convert_fusion.11, bf16[256,2048]{0,1:T(8,128)(2,1)} %get-tuple-element.461, bf16[1,64,2048]{2,1,0:T(8,128)(2,1)} %get-tuple-element.465, bf16[1,64,256]{2,1,0:T(8,128)(2,1)} %get-tuple-element.464), kind=kOutput, calls=%fused_computation.50.clone.1 | convolution fusion | flops 135806976 | bytes 1638400 | tf_op jit(solution)/shard_map/while/body/eval_jaxpr/kmn,kcn->kmc/dot_general | solution.py:67
  104.9 2.1 %fusion.131 = bf16[256,64]{0,1:T(8,128)(2,1)S(1)} fusion(bf16[64,2048]{1,0:T(8,128)(2,1)S(1)} %convolution_convert_fusion.11, bf16[256,2048]{0,1:T(8,128)(2,1)} %get-tuple-element.461, bf16[1,64,2048]{2,1,0:T(8,128)(2,1)} %get-tuple-element.465, bf16[1,64,256]{2,1,0:T(8,128)(2,1)} %get-tuple-element.464), kind=kOutput, calls=%fused_computation.50.clone.1 | convolution fusion | flops 135806976 | bytes 1638400 | tf_op jit(solution)/shard_map/while/body/eval_jaxpr/kmn,kcn->kmc/dot_general | solution.py:67
  108.2 2.1 %fusion.131 = bf16[256,64]{0,1:T(8,128)(2,1)S(1)} fusion(bf16[64,2048]{1,0:T(8,128)(2,1)S(1)} %convolution_convert_fusion.11, bf16[256,2048]{0,1:T(8,128)(2,1)} %get-tuple-element.461, bf16[1,64,2048]{2,1,0:T(8,128)(2,1)} %get-tuple-element.465, bf16[1,64,256]{2,1,0:T(8,128)(2,1)} %get-tuple-element.464), kind=kOutput, calls=%fused_computation.50.clone.1 | convolution fusion | flops 135806976 | bytes 1638400 | tf_op jit(solution)/shard_map/while/body/eval_jaxpr/kmn,kcn->kmc/dot_general | solution.py:67
  111.2 12.4 %collective-permute-start.4 = (bf16[1,64,2048]{2,1,0:T(8,128)(2,1)}, bf16[1,64,2048]{2,1,0:T(8,128)(2,1)S(1)}, u32[]{:S(2)}, u32[]{:S(2)}) collective-permute-start(bf16[1,64,2048]{2,1,0:T(8,128)(2,1)} %bitcast.48), channel_id=1, source_target_pairs={{0,504},{8,0},{16,8},{24,16},{32,24},{40,32},{48,40},{56,48},{64,5... | collective-permute-start | bytes 786440 | tf_op jit(solution)/shard_map/ppermute | solution.py:27
  123.6 9.7 %while.42 = (s32[]{:T(128)}, f32[3,1,64,64]{2,3,1,0:T(8,128)S(1)}, bf16[256,2048]{0,1:T(8,128)(2,1)}, bf16[3,1,64,64]{3,2,1,0:T(8,128)(2,1)S(1)}, bf16[1,64,2048...) while((s32[]{:T(128)}, f32[3,1,64,64]{2,3,1,0:T(8,128)S(1)}, ...), condition=%wide.region_5.6_spmd, body=%wide.region_4.5_spmd.sunk | while | flops 154812416 | bytes 2277485 | solution.py:72
  123.8 2.1 %fusion.122 = bf16[256,64]{0,1:T(8,128)(2,1)S(1)} fusion(bf16[64,2048]{1,0:T(8,128)(2,1)S(1)} %convolution_convert_fusion.10, bf16[256,2048]{0,1:T(8,128)(2,1)} %get-tuple-element.488, bf16[1,64,2048]{2,1,0:T(8,128)(2,1)} %get-tuple-element.492, bf16[1,64,256]{2,1,0:T(8,128)(2,1)} %get-tuple-element.491), kind=kOutput, calls=%fused_computation.35.clone.1 | convolution fusion | flops 135806976 | bytes 1638400 | tf_op jit(solution)/shard_map/while/body/eval_jaxpr/kmn,kcn->kmc/dot_general | solution.py:67
  127.1 2.1 %fusion.122 = bf16[256,64]{0,1:T(8,128)(2,1)S(1)} fusion(bf16[64,2048]{1,0:T(8,128)(2,1)S(1)} %convolution_convert_fusion.10, bf16[256,2048]{0,1:T(8,128)(2,1)} %get-tuple-element.488, bf16[1,64,2048]{2,1,0:T(8,128)(2,1)} %get-tuple-element.492, bf16[1,64,256]{2,1,0:T(8,128)(2,1)} %get-tuple-element.491), kind=kOutput, calls=%fused_computation.35.clone.1 | convolution fusion | flops 135806976 | bytes 1638400 | tf_op jit(solution)/shard_map/while/body/eval_jaxpr/kmn,kcn->kmc/dot_general | solution.py:67
  130.3 2.1 %fusion.122 = bf16[256,64]{0,1:T(8,128)(2,1)S(1)} fusion(bf16[64,2048]{1,0:T(8,128)(2,1)S(1)} %convolution_convert_fusion.10, bf16[256,2048]{0,1:T(8,128)(2,1)} %get-tuple-element.488, bf16[1,64,2048]{2,1,0:T(8,128)(2,1)} %get-tuple-element.492, bf16[1,64,256]{2,1,0:T(8,128)(2,1)} %get-tuple-element.491), kind=kOutput, calls=%fused_computation.35.clone.1 | convolution fusion | flops 135806976 | bytes 1638400 | tf_op jit(solution)/shard_map/while/body/eval_jaxpr/kmn,kcn->kmc/dot_general | solution.py:67
  133.4 8.6 %while.40 = (s32[]{:T(128)}, f32[3,1,64,64]{2,3,1,0:T(8,128)S(1)}, bf16[256,2048]{0,1:T(8,128)(2,1)S(1)}, bf16[3,1,64,64]{3,2,1,0:T(8,128)(2,1)S(1)}, bf16[1,64,...) while((s32[]{:T(128)}, f32[3,1,64,64]{2,3,1,0:T(8,128)S(1)}, ...), condition=%wide.region_1.2_spmd, body=%wide.region_0.1_spmd.sunk | while | flops 154812416 | bytes 2277485 | solution.py:72
  142.0 8.6 %while.41 = (s32[]{:T(128)}, f32[3,1,64,64]{2,3,1,0:T(8,128)S(1)}, bf16[256,2048]{0,1:T(8,128)(2,1)S(1)}, bf16[3,1,64,64]{3,2,1,0:T(8,128)(2,1)S(1)}, bf16[1,64,...) while((s32[]{:T(128)}, f32[3,1,64,64]{2,3,1,0:T(8,128)S(1)}, ...), condition=%wide.region_3.4_spmd, body=%wide.region_2.3_spmd.sunk | while | flops 154812416 | bytes 2277485 | solution.py:72
  150.9 27.8 %all_to_all.16 = f32[8,3,1,512]{3,2,1,0:T(1,128)S(1)} all-to-all(f32[8,3,1,512]{3,2,1,0:T(1,128)S(1)} %copy.25), channel_id=1, replica_groups=mesh['ka'=64,'mu'=8] {'mu'}, dimensions={0} | all-to-all | bytes 98304 | tf_op jit(solution)/shard_map/all_to_all | solution.py:37
  (70 shorter events, 37.7 us)
Async XLA Ops:
  33.7 32.8 %all-to-all-start.1 = ((bf16[8,1,64,256]{3,2,1,0:T(8,128)(2,1)}), bf16[8,1,64,256]{3,2,1,0:T(8,128)(2,1)S(1)}, u32[]{:S(2)}, u32[]{:S(2)}) async-start(bf16[8,1,64,256]{3,2,1,0:T(8,128)(2,1)} %broadcast_in_dim.69), calls=%async_computation.1 | async-start | bytes 524288 | tf_op jit(solution)/shard_map/all_to_all | solution.py:17
  38.4 28.7 %collective-permute-start.9 = (bf16[3,1,4096]{2,0,1:T(4,128)(2,1)S(1)}, bf16[3,1,4096]{2,0,1:T(4,128)(2,1)S(1)}, u32[]{:S(2)}, u32[]{:S(2)}) collective-permute-start(bf16[3,1,4096]{2,0,1:T(4,128)(2,1)S(1)} %bitcast.242), channel_id=1, source_target_pairs={{0,496},{8,504},{16,0},{24,8},{32,16},{40,24},{48,32},{56,40},{64,... | collective-permute-start | bytes 73736 | tf_op jit(solution)/shard_map/ppermute | solution.py:27
  46.3 51.3 %collective-permute-start.11 = (bf16[1,64,256]{2,1,0:T(8,128)(2,1)}, bf16[1,64,256]{2,1,0:T(8,128)(2,1)}, u32[]{:S(2)}, u32[]{:S(2)}) collective-permute-start(bf16[1,64,256]{2,1,0:T(8,128)(2,1)} %param.14), channel_id=1, source_target_pairs={{0,496},{8,504},{16,0},{24,8},{32,16},{40,24},{48,32},{56,40},{64,... | collective-permute-start | bytes 98312 | tf_op jit(solution)/shard_map/ppermute | solution.py:27
  49.0 29.2 %collective-permute-start.6 = (bf16[3,1,4096]{2,0,1:T(4,128)(2,1)S(1)}, bf16[3,1,4096]{2,0,1:T(4,128)(2,1)S(1)}, u32[]{:S(2)}, u32[]{:S(2)}) collective-permute-start(bf16[3,1,4096]{2,0,1:T(4,128)(2,1)S(1)} %bitcast.243), channel_id=1, source_target_pairs={{0,16},{8,24},{16,32},{24,40},{32,48},{40,56},{48,64},{56,72},{64,... | collective-permute-start | bytes 73736 | tf_op jit(solution)/shard_map/ppermute | solution.py:27
  52.2 29.3 %collective-permute-start = (bf16[3,1,4096]{2,0,1:T(4,128)(2,1)S(1)}, bf16[3,1,4096]{2,0,1:T(4,128)(2,1)}, u32[]{:S(2)}, u32[]{:S(2)}) collective-permute-start(bf16[3,1,4096]{2,0,1:T(4,128)(2,1)S(1)} %bitcast.244), channel_id=1, source_target_pairs={{0,8},{8,16},{16,24},{24,32},{32,40},{40,48},{48,56},{56,64},{64,7... | collective-permute-start | bytes 73736 | tf_op jit(solution)/shard_map/ppermute | solution.py:27
  54.1 30.2 %collective-permute-start.3 = (bf16[3,1,4096]{2,0,1:T(4,128)(2,1)S(1)}, bf16[3,1,4096]{2,0,1:T(4,128)(2,1)}, u32[]{:S(2)}, u32[]{:S(2)}) collective-permute-start(bf16[3,1,4096]{2,0,1:T(4,128)(2,1)S(1)} %bitcast.245), channel_id=1, source_target_pairs={{0,504},{8,0},{16,8},{24,16},{32,24},{40,32},{48,40},{56,48},{64,5... | collective-permute-start | bytes 73736 | tf_op jit(solution)/shard_map/ppermute | solution.py:27
  67.2 32.3 %collective-permute-start.10 = (bf16[1,64,2048]{2,1,0:T(8,128)(2,1)}, bf16[1,64,2048]{2,1,0:T(8,128)(2,1)S(1)}, u32[]{:S(2)}, u32[]{:S(2)}) collective-permute-start(bf16[1,64,2048]{2,1,0:T(8,128)(2,1)} %bitcast.48), channel_id=1, source_target_pairs={{0,496},{8,504},{16,0},{24,8},{32,16},{40,24},{48,32},{56,40},{64,... | collective-permute-start | bytes 786440 | tf_op jit(solution)/shard_map/ppermute | solution.py:27
  78.3 32.9 %collective-permute-start.8 = (bf16[1,64,256]{2,1,0:T(8,128)(2,1)}, bf16[1,64,256]{2,1,0:T(8,128)(2,1)S(1)}, u32[]{:S(2)}, u32[]{:S(2)}) collective-permute-start(bf16[1,64,256]{2,1,0:T(8,128)(2,1)} %param.14), channel_id=1, source_target_pairs={{0,16},{8,24},{16,32},{24,40},{32,48},{40,56},{48,64},{56,72},{64,... | collective-permute-start | bytes 98312 | tf_op jit(solution)/shard_map/ppermute | solution.py:27
  81.5 51.8 %collective-permute-start.2 = (bf16[1,64,256]{2,1,0:T(8,128)(2,1)}, bf16[1,64,256]{2,1,0:T(8,128)(2,1)}, u32[]{:S(2)}, u32[]{:S(2)}) collective-permute-start(bf16[1,64,256]{2,1,0:T(8,128)(2,1)} %param.14), channel_id=1, source_target_pairs={{0,8},{8,16},{16,24},{24,32},{32,40},{40,48},{48,56},{56,64},{64,7... | collective-permute-start | bytes 98312 | tf_op jit(solution)/shard_map/ppermute | solution.py:27
  84.3 57.7 %collective-permute-start.5 = (bf16[1,64,256]{2,1,0:T(8,128)(2,1)}, bf16[1,64,256]{2,1,0:T(8,128)(2,1)S(1)}, u32[]{:S(2)}, u32[]{:S(2)}) collective-permute-start(bf16[1,64,256]{2,1,0:T(8,128)(2,1)} %param.14), channel_id=1, source_target_pairs={{0,504},{8,0},{16,8},{24,16},{32,24},{40,32},{48,40},{56,48},{64,5... | collective-permute-start | bytes 98312 | tf_op jit(solution)/shard_map/ppermute | solution.py:27
  97.6 26.0 %collective-permute-start.7 = (bf16[1,64,2048]{2,1,0:T(8,128)(2,1)}, bf16[1,64,2048]{2,1,0:T(8,128)(2,1)S(1)}, u32[]{:S(2)}, u32[]{:S(2)}) collective-permute-start(bf16[1,64,2048]{2,1,0:T(8,128)(2,1)} %bitcast.48), channel_id=1, source_target_pairs={{0,16},{8,24},{16,32},{24,40},{32,48},{40,56},{48,64},{56,72},{64,... | collective-permute-start | bytes 786440 | tf_op jit(solution)/shard_map/ppermute | solution.py:27
  99.5 33.9 %collective-permute-start.1 = (bf16[1,64,2048]{2,1,0:T(8,128)(2,1)}, bf16[1,64,2048]{2,1,0:T(8,128)(2,1)S(1)}, u32[]{:S(2)}, u32[]{:S(2)}) collective-permute-start(bf16[1,64,2048]{2,1,0:T(8,128)(2,1)} %bitcast.48), channel_id=1, source_target_pairs={{0,8},{8,16},{16,24},{24,32},{32,40},{40,48},{48,56},{56,64},{64,7... | collective-permute-start | bytes 786440 | tf_op jit(solution)/shard_map/ppermute | solution.py:27
  111.2 12.4 %copy-start = (bf16[1,64,256]{2,1,0:T(8,128)(2,1)}, bf16[1,64,256]{2,1,0:T(8,128)(2,1)S(1)}, u32[]{:S(2)}) copy-start(bf16[1,64,256]{2,1,0:T(8,128)(2,1)S(1)} %collective-permute-done.8) | copy-start | bytes 98308
  111.2 30.8 %collective-permute-start.4 = (bf16[1,64,2048]{2,1,0:T(8,128)(2,1)}, bf16[1,64,2048]{2,1,0:T(8,128)(2,1)S(1)}, u32[]{:S(2)}, u32[]{:S(2)}) collective-permute-start(bf16[1,64,2048]{2,1,0:T(8,128)(2,1)} %bitcast.48), channel_id=1, source_target_pairs={{0,504},{8,0},{16,8},{24,16},{32,24},{40,32},{48,40},{56,48},{64,5... | collective-permute-start | bytes 786440 | tf_op jit(solution)/shard_map/ppermute | solution.py:27
where the time goes:
time: 181 us; the launch traced here: 179 us
  starting transfers between devices  69.1 us (38%)
  blocking collectives  59.3 us (33%)
  matrix products  36.5 us (20%)
  local copies, waits for them, and re-layouts  13.3 us (7%)
    ppermute x12, starting transfers between devices, passed_along(): return lax.ppermute(value, axis, pairs)  64.3 us
    all_to_all x1, blocking collectives, sent_to_all(): return lax.all_to_all(copies, axis, split_axis=0, concat_axis=0, tiled=True)  31.5 us
    all_to_all x1, blocking collectives, sum_at_owner(): lax.all_to_all(pieces, axis, split_axis=0, concat_axis=0, tiled=True)  27.8 us
    dot_general x12, matrix products, per_vector(): jnp.einsum('kmn,kcn->kmc', weighted, con_home, preferred_element_type=jnp...  23.3 us
    dot_general x12, matrix products, per_vector(): jnp.einsum('kvm,kmc->kvc', phi_val, folded, preferred_element_type=jnp.fl...  10.6 us
    all_to_all x1, starting transfers between devices, sent_to_all(): return lax.all_to_all(copies, axis, split_axis=0, concat_axis=0, tiled=True)  4.78 us
    unnamed x7, local copies, waits for them, and re-layouts  4.66 us
  transfers between devices with their start and end apart: 13, of which 0 were waited for; matrix products, arithmetic and copies ran while one was open for 22% of the time, Pallas kernels for 0%

commit v1 on v0

v1 whole, which is shorter than its diff:
```python
import functools

import jax
import jax.numpy as jnp
from jax import lax
from jax.experimental import pallas as pl
from jax.experimental.pallas import tpu as pltpu
from jax.sharding import PartitionSpec as P

MESH = pl.DeviceIdType.MESH
STEPS = (1, -1, 2, -2)
F32 = jnp.float32
BF16 = jnp.bfloat16


def kernel(
    vec_hbm, val_hbm, con_hbm, scr_hbm, out_ref,
    vec, xbuf, xall, xpart, con_own, con_part, val_own, val_part, scr, yv, fold, fcat, rbuf, rin,
    load_sem, send_sem, rx, rxp, rval, rnear, rfar, rp, rout,
):
    nk = lax.axis_size("ka")
    nmu = lax.axis_size("mu")
    k = lax.axis_index("ka")
    mu = lax.axis_index("mu")
    y, zh = mu // 2, mu % 2

    def wrapped(s):
        whole = (k + s + nk) // nk
        return whole - 1 if s > 0 else 1 - whole

    def ka_of(s):
        return lax.rem(k + s + nk, nk)

    loads = [
        pltpu.make_async_copy(vec_hbm, vec, load_sem.at[0]),
        pltpu.make_async_copy(con_hbm.at[0], con_own.at[zh, y], load_sem.at[1]),
        pltpu.make_async_copy(val_hbm.at[0], val_own, load_sem.at[2]),
    ] + [pltpu.make_async_copy(scr_hbm.at[o], scr.at[o], load_sem.at[3 + o]) for o in range(4)]

    barrier = pltpu.get_barrier_semaphore()
    for d in range(1, nmu):
        pl.semaphore_signal(barrier, inc=1, device_id={"mu": lax.rem(mu + d, nmu)}, device_id_type=MESH)
    for s in STEPS:
        pl.semaphore_signal(barrier, inc=1, device_id={"ka": ka_of(s)}, device_id_type=MESH)
        pl.semaphore_signal(
            barrier, inc=1, device_id={"ka": ka_of(s), "mu": 2 * y + lax.rem(zh + wrapped(s), 2)}, device_id_type=MESH
        )
    for load in loads:
        load.start()
    loads[0].wait()
    xbuf[...] = jnp.zeros_like(xbuf)
    for s in range(3):
        for r in range(8):
            xbuf[r : r + 1, s * 64 : (s + 1) * 64] = vec[s, :, r * 64 : (r + 1) * 64]
    xall[mu] = xbuf[...].astype(BF16)
    loads[1].wait()
    loads[2].wait()
    pl.semaphore_wait(barrier, nmu - 1 + 8)

    sent = []

    def send(src, dst, recv, device):
        copy = pltpu.make_async_remote_copy(
            src_ref=src, dst_ref=dst, send_sem=send_sem.at[len(sent)], recv_sem=recv,
            device_id=device, device_id_type=MESH,
        )
        copy.start()
        sent.append(copy)

    def arrived(ref, recv):
        pltpu.make_async_remote_copy(
            src_ref=ref, dst_ref=ref, send_sem=send_sem.at[0], recv_sem=recv,
            device_id={"mu": lax.rem(mu + 1, nmu)}, device_id_type=MESH,
        ).wait_recv()

    def to_partners_near(yy):
        for o, s in enumerate(STEPS):
            src = con_own.at[zh, yy]
            send(src, con_part.at[o, zh, yy], rp.at[0, o, yy], {"ka": ka_of(s)})

    def to_partners_far(yy):
        for o, s in enumerate(STEPS):
            w = wrapped(s)
            half = lax.rem(zh + 1 + w, 2)
            send(
                con_own.at[half, yy], con_part.at[o, half, yy], rp.at[1, o, yy],
                {"ka": ka_of(s), "mu": 2 * y + lax.rem(zh + w, 2)},
            )

    zo = 1 - zh
    for d in range(1, nmu):
        peer = lax.rem(mu + d, nmu)
        send(xall.at[mu], xall.at[mu], rx.at[mu], {"mu": peer})
    send(con_own.at[zh, y], con_own.at[zh, y], rfar.at[y], {"mu": 2 * y + zo})
    for d in range(1, 4):
        send(con_own.at[zh, y], con_own.at[zh, y], rnear.at[y], {"mu": 2 * lax.rem(y + d, 4) + zh})
    for o, s in enumerate(STEPS):
        send(val_own, val_part.at[o], rval.at[o], {"ka": ka_of(s)})
    to_partners_near(y)
    for d in (1, 3, 2):
        yy = lax.rem(y + d, 4)
        arrived(con_own.at[zh, yy], rnear.at[yy])
        to_partners_near(yy)
    for d in range(1, nmu):
        peer = lax.rem(mu + d, nmu)
        arrived(xall.at[peer], rx.at[peer])
    for o, s in enumerate(STEPS):
        send(xall, xpart.at[o], rxp.at[o], {"ka": ka_of(s), "mu": 2 * y + lax.rem(zh + wrapped(s), 2)})
    arrived(con_own.at[zo, y], rfar.at[y])
    for d in range(1, 4):
        send(con_own.at[zo, y], con_own.at[zo, y], rfar.at[y], {"mu": 2 * lax.rem(y + d, 4) + zh})
    to_partners_far(y)
    for d in (1, 3, 2):
        yy = lax.rem(y + d, 4)
        arrived(con_own.at[zo, yy], rfar.at[yy])
        to_partners_far(yy)

    for o in range(4):
        arrived(xpart.at[o], rxp.at[o])
        arrived(val_part.at[o], rval.at[o])
        x = xpart[o].astype(F32).reshape(64, 256).astype(BF16)
        for s in range(3):
            part = lax.dot_general(
                val_part[o], x[:, s * 64 : (s + 1) * 64], (((0,), (0,)), ((), ())), preferred_element_type=F32
            )
            yv[o, s * 256 : (s + 1) * 256, :] = part.astype(BF16)
    fold[...] = jnp.zeros_like(fold)
    for load in loads[3:]:
        load.wait()

    def block(i, carry):
        phase = i // 4
        half = lax.rem(zh + phase, 2)
        yy = lax.rem(y + i, 4)
        for o in range(4):
            arrived(con_part.at[o, half, yy], rp.at[phase, o, yy])
        columns = pl.ds(pl.multiple_of((2 * yy + half) * 256, 256), 256)
        for s in range(3):
            rows = slice(s * 256, (s + 1) * 256)
            total = None
            for o in range(4):
                paired = jnp.dot(yv[o, rows, :], con_part[o, half, yy], preferred_element_type=F32)
                term = scr[o, :, columns].astype(F32) * paired
                total = term if total is None else total + term
            fold[rows, :] += lax.dot_general(
                total.astype(BF16), con_own[half, yy], (((1,), (1,)), ((), ())), preferred_element_type=F32
            )
        return carry

    lax.fori_loop(0, 8, block, 0)

    for s in range(3):
        fcat[:, s * 64 : (s + 1) * 64] = fold[s * 256 : (s + 1) * 256, :].astype(BF16)
    result = jnp.dot(val_own[...], fcat[...], preferred_element_type=F32)
    for j in range(8):
        rbuf[j] = result[j * 8 : (j + 1) * 8, :].astype(BF16)
    for d in range(1, nmu):
        peer = lax.rem(mu + d, nmu)
        send(rbuf.at[peer], rin.at[mu], rout.at[mu], {"mu": peer})
    total = rbuf[mu].astype(F32)
    for d in range(1, nmu):
        peer = lax.rem(mu + d, nmu)
        arrived(rin.at[peer], rout.at[peer])
        total = total + rin[peer].astype(F32)
    out_ref[...] = total
    for copy in sent:
        copy.wait_send()


def local(vectors, phi_val, phi_con, screened, partner):
    anyspace = pl.BlockSpec(memory_space=pl.ANY)
    dma = pltpu.SemaphoreType.DMA
    out = pl.pallas_call(
        kernel,
        out_shape=jax.ShapeDtypeStruct((8, 256), F32),
        in_specs=[anyspace] * 4,
        out_specs=pl.BlockSpec(memory_space=pltpu.VMEM),
        scratch_shapes=[
            pltpu.VMEM((3, 1, 512), F32),
            pltpu.VMEM((8, 256), F32),
            pltpu.VMEM((8, 8, 256), BF16),
            pltpu.VMEM((4, 8, 8, 256), BF16),
            pltpu.VMEM((2, 4, 64, 256), BF16),
            pltpu.VMEM((4, 2, 4, 64, 256), BF16),
            pltpu.VMEM((64, 256), BF16),
            pltpu.VMEM((4, 64, 256), BF16),
            pltpu.VMEM((4, 256, 2048), BF16),
            pltpu.VMEM((4, 768, 64), BF16),
            pltpu.VMEM((768, 64), F32),
            pltpu.VMEM((256, 256), BF16),
            pltpu.VMEM((8, 8, 256), BF16),
            pltpu.VMEM((8, 8, 256), BF16),
            dma((7,)),
            dma((64,)),
            dma((8,)),
            dma((4,)),
            dma((4,)),
            dma((4,)),
            dma((4,)),
            dma((2, 4, 4)),
            dma((8,)),
        ],
        compiler_params=pltpu.CompilerParams(collective_id=0, has_side_effects=True),
        name="isdf_direct",
    )(vectors, phi_val, phi_con, screened)
    return out[:, :192].reshape(8, 3, 64).transpose(1, 0, 2).reshape(3, 1, 512)


def solution(mesh):
    placed = (
        P(None, "ka", "mu"),
        P("ka", None, "mu"),
        P("ka", None, "mu"),
        P(None, "mu", None),
        P("ka", None),
    )
    return jax.shard_map(
        local, mesh=mesh, in_specs=placed, out_specs=P(None, "ka", "mu"), check_vma=False
    )
```

time: 181 us -> 51.9 us (0.29)
  the two profiles are of different devices: /device:TPU:8 before, /device:TPU:1 now
where the time goes in v1:
time: 51.9 us; the launch traced here: 51.7 us
  Pallas kernels  50.3 us (97%)
  local copies, waits for them, and re-layouts  1.45 us (3%)
    pallas_call x1, Pallas kernels, local(): pl.pallas_call(kernel, out_shape=jax.ShapeDtypeStruct((8, 256), F32), in_...  50.3 us
    reshape x2, local copies, waits for them, and re-layouts, local(): return out[:, :192].reshape(8, 3, 64).transpose(1, 0, 2).reshape(3, 1, 512)  1.45 us

profile of v1, /device:TPU:1, one launch (start us, length us, event | category | flops | bytes accessed | tf_op | source)
XLA Modules:
  0.0 51.7 jit_solution(1862872359421390072)
XLA Ops:
  0.0 50.3 %isdf_direct.1 = f32[8,256]{1,0:T(8,128)} custom-call(f32[3,1,512]{2,1,0:T(1,128)} %vec_hbm.1, bf16[1,64,256]{2,1,0:T(8,128)(2,1)} %val_hbm.1, bf16[1,64,256]{2,1,0:T(8,128)(2,1)} %con_hbm.1, bf16[4,256,2048]{2,1,0:T(8,128)(2,1)} %scr_hbm.1), custom_call_target="tpu_custom_call" | custom-call | tf_op jit(solution)/shard_map/isdf_direct/pallas_call | solution.py:173
  50.3 0.8 %reshape.6 = f32[8,3,64]{2,1,0:T(4,128)S(1)} reshape(f32[8,192]{1,0:T(8,128)} %bitcast.3) | data formatting | bytes 12288 | tf_op jit(solution)/shard_map/reshape | solution.py:206
  51.1 0.7 %reshape.8 = f32[3,1,512]{2,1,0:T(1,128)} reshape(f32[3,8,64]{2,1,0:T(8,128)S(1)} %copy.6) | data formatting | bytes 12288 | tf_op jit(solution)/shard_map/reshape | solution.py:206
  (1 shorter events, 0.0 us)
